TPU v7x, 512 devices: a whole 4x8x8 slice. The times are simulated.
512 devices in a mesh: section: 16 (over x_lo, z), latent: 32 (over x_hi, y, core).
Axes of the slice: x: 4 (x_hi: 2, x_lo: 2; x = x_hi * 2 + x_lo), y: 8, z: 8, core: 2. Of those that a mesh axis runs over, the one named last changes fastest.
Arguments:
- residual: bfloat16 [4, 320, 4608], P(None, None, 'latent'), may hold values from -6 to 6
- encoder: bfloat16 [16, 4608, 4096], P('section', None, 'latent'), may hold values from -0.09375 to 0.09375
- enc_bias: float32 [16, 4096], P('section', 'latent'), may hold values from -4 to 4
- gate_code: int32 [16, 4096], P('section', 'latent'), may hold values from 0 to 2
- decoder: bfloat16 [16, 3, 4096, 4608], P('section', None, 'latent'), may hold values from -0.0546875 to 0.0546875
Outputs:
- reconstruction: bfloat16 [16, 80, 4608], P('section', None, 'latent')
- latent_acts: bfloat16 [16, 320, 4096], P('section', None, 'latent')
Inputs may be any that keep to these rules, and one draw needn't show every extreme that they name: `gate_code`: 0: the latent is always active; 1: its threshold is zero; 2: it is never active.
All inputs are finite; a program needn't handle non-finite values.
Results may differ from a plain program's by a relative error of at most 0.019.
Values may be sent and summed in bfloat16 or wider, within the bound.
A program may use at most 64 MiB of HBM per device.

v0:
```python
import jax
import jax.numpy as jnp
from jax import lax
from jax.sharding import PartitionSpec as P

LAYERS = 4


def swapped(shard, axis, stride):
    return lax.ppermute(shard, axis, [(i, i ^ 1 << stride) for i in range(lax.axis_size(axis))])


def passed_along(value, axis, steps):
    count = lax.axis_size(axis)
    first, last = (max(0, -steps), min(count, count - steps))
    return lax.ppermute(value, axis, [(source, source + steps) for source in range(first, last)])


def group_reduce(partial_rows, group_size):
    current = partial_rows
    section_index = lax.axis_index("section")
    level_count = group_size.bit_length() - 1
    for level in reversed(range(level_count)):
        half = current.shape[0] // 2
        lower = current[:half]
        upper = current[half:]
        high_side = section_index // 2**level % 2 == 1
        kept = jnp.where(high_side, upper, lower)
        sent = jnp.where(high_side, lower, upper)
        received = swapped(sent.astype(jnp.bfloat16), "section", level).astype(sent.dtype)
        current = kept + received
    return current


def shards(residual, encoder, enc_bias, gate_code, decoder):
    group_size = lax.axis_size("section") // LAYERS
    layer_index = lax.axis_index("section") // group_size
    resid_layer = lax.dynamic_index_in_dim(residual, layer_index, 0, keepdims=False)
    enc_local = encoder[0]
    preact = jnp.dot(
        lax.all_gather(resid_layer, "latent", axis=1, tiled=True),
        enc_local,
        preferred_element_type=jnp.float32,
    )
    preact = preact + enc_bias[0]
    threshold = 10000.0 * (gate_code[0].astype(jnp.float32) - 1.0)
    active_vals = jnp.where(preact > threshold, preact, jnp.zeros_like(preact)).astype(jnp.bfloat16)
    reach_count = decoder.shape[1]
    sources = [active_vals]
    carried = active_vals
    for hop_index in range(1, reach_count):
        carried = passed_along(carried, "section", group_size)
        sources.append(carried)
    stacked = jnp.stack(sources, axis=0)
    dec_local = decoder[0]
    own_share = lax.psum_scatter(
        lax.dot_general(
            dec_local, stacked, (((0, 1), (0, 2)), ((), ())), preferred_element_type=jnp.float32
        ).astype(jnp.bfloat16),
        "latent",
        scatter_dimension=0,
        tiled=True,
    ).astype(jnp.float32)
    summed = jnp.transpose(own_share)
    rebuilt = group_reduce(summed, group_size).astype(jnp.bfloat16)
    return (rebuilt[None], active_vals[None])


def solution(mesh):
    return jax.shard_map(
        shards,
        mesh=mesh,
        in_specs=(
            P(None, None, "latent"),
            P("section", None, "latent"),
            P("section", "latent"),
            P("section", "latent"),
            P("section", None, "latent", None),
        ),
        out_specs=(P("section", None, "latent"), P("section", None, "latent")),
        check_vma=False,
    )
```

profile of v0, /device:TPU:16, one launch (start us, length us, event | category | flops | bytes accessed | tf_op | source)
XLA Modules:
  0.0 296.9 jit_solution(9694946097347359255)
XLA Ops:
  7.2 0.0 copy-start
  7.2 0.0 all-gather.3.cloned.1.call-start
  7.2 1.7 constant_dynamic-slice_fusion
  8.9 0.0 all-gather.3.cloned.1.call-update
  9.0 0.0 reduce-scatter.4.cloned.1.call-start
  9.0 0.7 multiply_bitcast_fusion
  9.7 94.1 %all-gather.3.cloned.1.call-done = bf16[1,320,4608]{1,2,0:T(8,128)(2,1)} async-done(((bf16[1,320,144]{1,2,0:T(8,128)(2,1)}), bf16[1,320,4608]{1,2,0:T(8,128)(2,1)}) %all-gather.3.cloned.1.call-update) | async-done | bytes 2949136 | tf_op jit(solution)/shard_map/all_gather | solution.py:41
  103.8 3.5 %fusion.15 = bf16[320,128]{1,0:T(8,128)(2,1)S(1)} fusion(bf16[1,4608,128]{2,1,0:T(8,128)(2,1)} %param.6, bf16[1,320,4608]{1,2,0:T(8,128)(2,1)} %all-gather.3.cloned.1.call-done, f32[128]{0:T(128)S(1)} %multiply_bitcast_fusion, f32[128]{0:T(128)} %bitcast.44), kind=kOutput, calls=%fused_computation.9 | convolution fusion | flops 377651200 | bytes 4211712 | tf_op jit(solution)/shard_map/dot_general | solution.py:40
  107.3 0.0 copy-start.2
  107.3 8.0 %collective-permute-start = (bf16[320,128]{1,0:T(8,128)(2,1)S(1)}, bf16[320,128]{1,0:T(8,128)(2,1)S(1)}, u32[]{:S(2)}, u32[]{:S(2)}) collective-permute-start(bf16[320,128]{1,0:T(8,128)(2,1)S(1)} %fusion.15), channel_id=1, source_target_pairs={{0,128},{32,160},{64,192},{96,224},{128,256},{160,288},{192,320},{... | collective-permute-start | bytes 245768 | tf_op jit(solution)/shard_map/ppermute | solution.py:16
  115.3 2.1 collective-permute-done
  117.5 9.9 %collective-permute-start.1 = (bf16[320,128]{1,0:T(8,128)(2,1)S(1)}, bf16[320,128]{1,0:T(8,128)(2,1)S(1)}, u32[]{:S(2)}, u32[]{:S(2)}) collective-permute-start(bf16[320,128]{1,0:T(8,128)(2,1)S(1)} %collective-permute-done), channel_id=1, source_target_pairs={{0,128},{32,160},{64,192},{96,224},{128,256},{160,288},{192,320},{... | collective-permute-start | bytes 245768 | tf_op jit(solution)/shard_map/ppermute | solution.py:16
  127.3 3.7 %collective-permute-done.1 = bf16[320,128]{1,0:T(8,128)(2,1)S(1)} collective-permute-done((bf16[320,128]{1,0:T(8,128)(2,1)S(1)}, bf16[320,128]{1,0:T(8,128)(2,1)S(1)}, u32[]{:S(2)}, u32[]{:S(2)}) %collective-permute-start.1) | collective-permute-done | bytes 81952 | tf_op jit(solution)/shard_map/ppermute | solution.py:16
  131.0 0.0 copy-done.2
  131.0 0.0 copy-done
  131.0 3.3 %fusion.1 = bf16[4608,320]{0,1:T(8,128)(2,1)} fusion(bf16[1,3,128,4608]{3,2,1,0:T(8,128)(2,1)S(1)} %copy-done, bf16[1,320,128]{2,1,0:T(8,128)(2,1)S(1)} %bitcast.43, bf16[1,320,128]{2,1,0:T(8,128)(2,1)S(1)} %bitcast.42, bf16[1,320,128]{2,1,0:T(8,128)(2,1)S(1)} %bitcast.40), kind=kOutput, calls=%fused_computation.2 | convolution fusion | flops 1134182400 | bytes 6733824 | tf_op jit(solution)/shard_map/dot_general | solution.py:57
  134.3 5.5 %copy.9 = bf16[4608,320]{1,0:T(8,128)(2,1)} copy(bf16[4608,320]{0,1:T(8,128)(2,1)} %fusion.1) | data formatting | bytes 5898240
  139.8 0.0 reduce-scatter.4.cloned.1.call-update
  139.9 129.5 %reduce-scatter.4.cloned.1.call-done = bf16[144,320]{1,0:T(8,128)(2,1)} async-done(((bf16[4608,320]{1,0:T(8,128)(2,1)}), bf16[144,320]{1,0:T(8,128)(2,1)}) %reduce-scatter.4.cloned.1.call-update) | async-done | bytes 92176
  269.4 1.7 copy.10
  271.0 0.9 convert_bitcast_fusion
  272.0 0.0 copy-start.1
  272.0 0.7 copy-done.1
  272.7 0.7 select_convert_fusion
  273.4 4.6 %collective-permute-start.2 = (bf16[160,144]{1,0:T(8,128)(2,1)}, bf16[160,144]{1,0:T(8,128)(2,1)}, u32[]{:S(2)}, u32[]{:S(2)}) collective-permute-start(bf16[160,144]{1,0:T(8,128)(2,1)} %select_convert_fusion), channel_id=1, source_target_pairs={{0,64},{32,96},{64,0},{96,32},{128,192},{160,224},{192,128},{224,1... | collective-permute-start | bytes 138248 | tf_op jit(solution)/shard_map/ppermute | solution.py:10
  278.0 2.9 collective-permute-done.2
  280.9 1.1 convert_add_fusion
  282.0 3.6 %collective-permute-start.3 = (bf16[80,144]{1,0:T(8,128)(2,1)S(1)}, bf16[80,144]{1,0:T(8,128)(2,1)S(1)}, u32[]{:S(2)}, u32[]{:S(2)}) collective-permute-start(bf16[80,144]{1,0:T(8,128)(2,1)S(1)} %select_convert_fusion.1), channel_id=1, source_target_pairs={{0,32},{32,0},{64,96},{96,64},{128,160},{160,128},{192,224},{224,1... | collective-permute-start | bytes 69128 | tf_op jit(solution)/shard_map/ppermute | solution.py:10
  285.6 2.3 collective-permute-done.3
  287.9 0.6 fusion.25
  288.5 1.5 copy.8
  (1 shorter events, 0.0 us)
Async XLA Ops:
  7.2 123.9 %copy-start = (bf16[1,3,128,4608]{3,2,1,0:T(8,128)(2,1)S(1)}, bf16[1,3,128,4608]{3,2,1,0:T(8,128)(2,1)}, u32[]{:S(2)}) copy-start(bf16[1,3,128,4608]{3,2,1,0:T(8,128)(2,1)} %param.9) | copy-start | bytes 10616836
  7.2 96.6 %all-gather.3.cloned.1.call-start = ((), (), s32[]{:S(2)}) async-start(), calls=%async_computation.1 | async-start | bytes 3649536 | tf_op jit(solution)/shard_map/all_gather | solution.py:41
  9.0 260.4 %reduce-scatter.4.cloned.1.call-start = ((), (), s32[]{:S(2)}) async-start(), calls=%async_computation.2 | async-start | bytes 3649536
  107.3 23.7 %copy-start.2 = (bf16[320,128]{1,0:T(8,128)(2,1)}, bf16[320,128]{1,0:T(8,128)(2,1)S(1)}, u32[]{:S(2)}) copy-start(bf16[320,128]{1,0:T(8,128)(2,1)S(1)} %fusion.15) | copy-start | bytes 245764
  107.3 10.2 %collective-permute-start = (bf16[320,128]{1,0:T(8,128)(2,1)S(1)}, bf16[320,128]{1,0:T(8,128)(2,1)S(1)}, u32[]{:S(2)}, u32[]{:S(2)}) collective-permute-start(bf16[320,128]{1,0:T(8,128)(2,1)S(1)} %fusion.15), channel_id=1, source_target_pairs={{0,128},{32,160},{64,192},{96,224},{128,256},{160,288},{192,320},{... | collective-permute-start | bytes 245768 | tf_op jit(solution)/shard_map/ppermute | solution.py:16
  117.5 13.6 %collective-permute-start.1 = (bf16[320,128]{1,0:T(8,128)(2,1)S(1)}, bf16[320,128]{1,0:T(8,128)(2,1)S(1)}, u32[]{:S(2)}, u32[]{:S(2)}) collective-permute-start(bf16[320,128]{1,0:T(8,128)(2,1)S(1)} %collective-permute-done), channel_id=1, source_target_pairs={{0,128},{32,160},{64,192},{96,224},{128,256},{160,288},{192,320},{... | collective-permute-start | bytes 245768 | tf_op jit(solution)/shard_map/ppermute | solution.py:16
  272.0 0.7 copy-start.1
  273.4 7.5 %collective-permute-start.2 = (bf16[160,144]{1,0:T(8,128)(2,1)}, bf16[160,144]{1,0:T(8,128)(2,1)}, u32[]{:S(2)}, u32[]{:S(2)}) collective-permute-start(bf16[160,144]{1,0:T(8,128)(2,1)} %select_convert_fusion), channel_id=1, source_target_pairs={{0,64},{32,96},{64,0},{96,32},{128,192},{160,224},{192,128},{224,1... | collective-permute-start | bytes 138248 | tf_op jit(solution)/shard_map/ppermute | solution.py:10
  282.0 5.9 %collective-permute-start.3 = (bf16[80,144]{1,0:T(8,128)(2,1)S(1)}, bf16[80,144]{1,0:T(8,128)(2,1)S(1)}, u32[]{:S(2)}, u32[]{:S(2)}) collective-permute-start(bf16[80,144]{1,0:T(8,128)(2,1)S(1)} %select_convert_fusion.1), channel_id=1, source_target_pairs={{0,32},{32,0},{64,96},{96,64},{128,160},{160,128},{192,224},{224,1... | collective-permute-start | bytes 69128 | tf_op jit(solution)/shard_map/ppermute | solution.py:10
Sparse Core Ops, SparseCore 0:
  11.3 92.4 all-gather.2
  140.0 129.3 reduce-scatter.3
where the time goes:
time: 297 us
  waiting for transfers between devices  235 us (79%)
  starting transfers between devices  26.2 us (9%)
  between operations  14.2 us (5%)
  local copies, waits for them, and re-layouts  11.1 us (4%)
  matrix products  6.78 us (2%)
  other arithmetic  3.95 us (1%)
    unnamed x3, waiting for transfers between devices  130 us
    all_gather x1, waiting for transfers between devices, shards(): lax.all_gather(resid_layer, 'latent', axis=1, tiled=True)  94.1 us
    ppermute x2, starting transfers between devices, passed_along(): lax.ppermute(value, axis, [(source, source + steps) for source in range(f...  17.9 us
    unnamed x9, local copies, waits for them, and re-layouts  9.42 us
    ppermute x2, starting transfers between devices, swapped(): lax.ppermute(shard, axis, [(i, i ^ 1 << stride) for i in range(lax.axis_s...  8.22 us
  transfers between devices with their start and end apart: 6, of which 6 were waited for; matrix products, arithmetic and copies ran while one was open for 0% of the time, Pallas kernels for 0%

commit v1 on v0

--- a/solution.py
+++ b/solution.py
@@ -37,11 +37,16 @@
     layer_index = lax.axis_index("section") // group_size
     resid_layer = lax.dynamic_index_in_dim(residual, layer_index, 0, keepdims=False)
     enc_local = encoder[0]
-    preact = jnp.dot(
-        lax.all_gather(resid_layer, "latent", axis=1, tiled=True),
-        enc_local,
-        preferred_element_type=jnp.float32,
+    _draw_spots = lambda body: jnp.concatenate(
+        lax.all_to_all(
+            jnp.stack([body] * lax.axis_size("latent"), axis=0),
+            axis_name="latent",
+            split_axis=0,
+            concat_axis=0,
+        ),
+        1,
     )
+    preact = jnp.dot(_draw_spots(resid_layer), enc_local, preferred_element_type=jnp.float32)
     preact = preact + enc_bias[0]
     threshold = 10000.0 * (gate_code[0].astype(jnp.float32) - 1.0)
     active_vals = jnp.where(preact > threshold, preact, jnp.zeros_like(preact)).astype(jnp.bfloat16)

time: 297 us -> 298 us (level)
  waiting for transfers between devices: 235 us -> 223 us
  starting transfers between devices: 26.2 us -> 38 us
    all_gather x1 -> x0, waiting for transfers between devices: 94.1 us -> none  [shards(): lax.all_gather(resid_layer, 'latent', axis=1, tiled=True)]
    all_to_all x0 -> x1, waiting for transfers between devices: none -> 78.1 us  [shards(): lax.all_to_all(jnp.stack([body] * lax.axis_size('latent'), axis=0), axis_...]
    all_to_all x0 -> x1, starting transfers between devices: none -> 10.2 us  [shards(): lax.all_to_all(jnp.stack([body] * lax.axis_size('latent'), axis=0), axis_...]
    unnamed x3 -> x2, waiting for transfers between devices: 130 us -> 133 us
    unnamed x9 -> x13, local copies, waits for them, and re-layouts: 9.42 us -> 9.43 us
where the time goes in v1:
time: 298 us
  waiting for transfers between devices  223 us (75%)
  starting transfers between devices  38 us (13%)
  between operations  14.2 us (5%)
  local copies, waits for them, and re-layouts  12.6 us (4%)
  matrix products  6.75 us (2%)
  other arithmetic  3.29 us (1%)
    unnamed x2, waiting for transfers between devices  133 us
    all_to_all x1, waiting for transfers between devices, shards(): lax.all_to_all(jnp.stack([body] * lax.axis_size('latent'), axis=0), axis_...  78.1 us
    ppermute x2, starting transfers between devices, passed_along(): lax.ppermute(value, axis, [(source, source + steps) for source in range(f...  19.5 us
    all_to_all x1, starting transfers between devices, shards(): lax.all_to_all(jnp.stack([body] * lax.axis_size('latent'), axis=0), axis_...  10.2 us
    unnamed x13, local copies, waits for them, and re-layouts  9.43 us
    ppermute x2, starting transfers between devices, swapped(): lax.ppermute(shard, axis, [(i, i ^ 1 << stride) for i in range(lax.axis_s...  8.29 us
    ppermute x2, waiting for transfers between devices, passed_along(): lax.ppermute(value, axis, [(source, source + steps) for source in range(f...  7.24 us
  transfers between devices with their start and end apart: 6, of which 6 were waited for; matrix products, arithmetic and copies ran while one was open for 0% of the time, Pallas kernels for 0%

profile of v1, /device:TPU:16, one launch (start us, length us, event | category | flops | bytes accessed | tf_op | source)
XLA Modules:
  0.0 297.9 jit_solution(5947142344105284638)
XLA Ops:
  7.2 0.0 copy-start
  7.2 1.1 dynamic-slice_bitcast_fusion
  8.3 2.1 stack.10
  10.4 0.0 copy-start.4
  10.4 0.0 copy-start.3
  10.4 10.2 %all-to-all-start = ((bf16[32,320,144]{1,2,0:T(8,128)(2,1)}), bf16[32,320,144]{1,2,0:T(8,128)(2,1)}, u32[]{:S(2)}, u32[]{:S(2)}) async-start(bf16[32,320,144]{1,2,0:T(8,128)(2,1)} %stack.10), calls=%async_computation | async-start | bytes 7077888 | tf_op jit(solution)/shard_map/all_to_all | solution.py:41
  20.6 0.0 reduce-scatter.4.cloned.1.call-start
  20.7 0.0 copy-done.4
  20.7 78.1 %all-to-all-done = bf16[32,320,144]{1,2,0:T(8,128)(2,1)} async-done(((bf16[32,320,144]{1,2,0:T(8,128)(2,1)}), bf16[32,320,144]{1,2,0:T(8,128)(2,1)}, u32[]{:S(2)}, u32[]{:S(2)}) %all-to-all-start) | async-done | bytes 2949152 | tf_op jit(solution)/shard_map/all_to_all | solution.py:41
  98.8 0.0 copy-done.3
  98.8 3.5 %fusion.10 = bf16[320,128]{1,0:T(8,128)(2,1)S(1)} fusion(bf16[320,4608]{0,1:T(8,128)(2,1)} %bitcast.2, bf16[1,4608,128]{2,1,0:T(8,128)(2,1)} %param.6, f32[128]{0:T(128)S(1)} %multiply_bitcast_fusion, f32[128]{0:T(128)S(1)} %bitcast.41), kind=kOutput, calls=%fused_computation.8 | convolution fusion | flops 377651200 | bytes 4211712 | tf_op jit(solution)/shard_map/dot_general | solution.py:49
  102.2 0.0 copy-start.2
  102.2 11.2 %collective-permute-start = (bf16[320,128]{1,0:T(8,128)(2,1)S(1)}, bf16[320,128]{1,0:T(8,128)(2,1)S(1)}, u32[]{:S(2)}, u32[]{:S(2)}) collective-permute-start(bf16[320,128]{1,0:T(8,128)(2,1)S(1)} %fusion.10), channel_id=1, source_target_pairs={{0,128},{32,160},{64,192},{96,224},{128,256},{160,288},{192,320},{... | collective-permute-start | bytes 245768 | tf_op jit(solution)/shard_map/ppermute | solution.py:16
  113.5 3.6 %collective-permute-done = bf16[320,128]{1,0:T(8,128)(2,1)S(1)} collective-permute-done((bf16[320,128]{1,0:T(8,128)(2,1)S(1)}, bf16[320,128]{1,0:T(8,128)(2,1)S(1)}, u32[]{:S(2)}, u32[]{:S(2)}) %collective-permute-start) | collective-permute-done | bytes 81952 | tf_op jit(solution)/shard_map/ppermute | solution.py:16
  117.1 8.3 %collective-permute-start.1 = (bf16[320,128]{1,0:T(8,128)(2,1)S(1)}, bf16[320,128]{1,0:T(8,128)(2,1)S(1)}, u32[]{:S(2)}, u32[]{:S(2)}) collective-permute-start(bf16[320,128]{1,0:T(8,128)(2,1)S(1)} %collective-permute-done), channel_id=1, source_target_pairs={{0,128},{32,160},{64,192},{96,224},{128,256},{160,288},{192,320},{... | collective-permute-start | bytes 245768 | tf_op jit(solution)/shard_map/ppermute | solution.py:16
  125.3 3.6 %collective-permute-done.1 = bf16[320,128]{1,0:T(8,128)(2,1)S(1)} collective-permute-done((bf16[320,128]{1,0:T(8,128)(2,1)S(1)}, bf16[320,128]{1,0:T(8,128)(2,1)S(1)}, u32[]{:S(2)}, u32[]{:S(2)}) %collective-permute-start.1) | collective-permute-done | bytes 81952 | tf_op jit(solution)/shard_map/ppermute | solution.py:16
  129.0 0.0 copy-done.2
  129.0 0.0 copy-done
  129.0 3.3 %fusion.1 = bf16[4608,320]{0,1:T(8,128)(2,1)} fusion(bf16[1,3,128,4608]{3,2,1,0:T(8,128)(2,1)S(1)} %copy-done, bf16[1,320,128]{2,1,0:T(8,128)(2,1)S(1)} %bitcast.40, bf16[1,320,128]{2,1,0:T(8,128)(2,1)S(1)} %bitcast.39, bf16[1,320,128]{2,1,0:T(8,128)(2,1)S(1)} %bitcast.37), kind=kOutput, calls=%fused_computation.2 | convolution fusion | flops 1134182400 | bytes 6733824 | tf_op jit(solution)/shard_map/dot_general | solution.py:62
  132.3 5.5 %copy.10 = bf16[4608,320]{1,0:T(8,128)(2,1)} copy(bf16[4608,320]{0,1:T(8,128)(2,1)} %fusion.1) | data formatting | bytes 5898240
  137.8 0.0 reduce-scatter.4.cloned.1.call-update
  137.8 132.6 %reduce-scatter.4.cloned.1.call-done = bf16[144,320]{1,0:T(8,128)(2,1)} async-done(((bf16[4608,320]{1,0:T(8,128)(2,1)}), bf16[144,320]{1,0:T(8,128)(2,1)}) %reduce-scatter.4.cloned.1.call-update) | async-done | bytes 92176
  270.4 1.7 copy.11
  272.1 0.9 convert_bitcast_fusion
  273.0 0.0 copy-start.1
  273.0 0.7 copy-done.1
  273.7 0.7 select_convert_fusion
  274.4 4.7 %collective-permute-start.2 = (bf16[160,144]{1,0:T(8,128)(2,1)}, bf16[160,144]{1,0:T(8,128)(2,1)}, u32[]{:S(2)}, u32[]{:S(2)}) collective-permute-start(bf16[160,144]{1,0:T(8,128)(2,1)} %select_convert_fusion), channel_id=1, source_target_pairs={{0,64},{32,96},{64,0},{96,32},{128,192},{160,224},{192,128},{224,1... | collective-permute-start | bytes 138248 | tf_op jit(solution)/shard_map/ppermute | solution.py:10
  279.1 2.9 collective-permute-done.2
  282.0 1.1 convert_add_fusion
  283.0 3.6 %collective-permute-start.3 = (bf16[80,144]{1,0:T(8,128)(2,1)S(1)}, bf16[80,144]{1,0:T(8,128)(2,1)S(1)}, u32[]{:S(2)}, u32[]{:S(2)}) collective-permute-start(bf16[80,144]{1,0:T(8,128)(2,1)S(1)} %select_convert_fusion.1), channel_id=1, source_target_pairs={{0,32},{32,0},{64,96},{96,64},{128,160},{160,128},{192,224},{224,1... | collective-permute-start | bytes 69128 | tf_op jit(solution)/shard_map/ppermute | solution.py:10
  286.7 2.3 collective-permute-done.3
  288.9 0.6 fusion.18
  289.6 1.5 copy.9
  (2 shorter events, 0.0 us)
Async XLA Ops:
  7.2 121.8 %copy-start = (bf16[1,3,128,4608]{3,2,1,0:T(8,128)(2,1)S(1)}, bf16[1,3,128,4608]{3,2,1,0:T(8,128)(2,1)}, u32[]{:S(2)}) copy-start(bf16[1,3,128,4608]{3,2,1,0:T(8,128)(2,1)} %param.9) | copy-start | bytes 10616836
  10.4 10.3 %copy-start.4 = (s32[1,128]{1,0:T(1,128)S(1)}, s32[1,128]{1,0:T(1,128)}, u32[]{:S(2)}) copy-start(s32[1,128]{1,0:T(1,128)} %param.8) | copy-start | bytes 1540
  10.4 88.4 %copy-start.3 = (f32[1,128]{1,0:T(1,128)S(1)}, f32[1,128]{1,0:T(1,128)}, u32[]{:S(2)}) copy-start(f32[1,128]{1,0:T(1,128)} %param.7) | copy-start | bytes 1540
  10.4 88.4 %all-to-all-start = ((bf16[32,320,144]{1,2,0:T(8,128)(2,1)}), bf16[32,320,144]{1,2,0:T(8,128)(2,1)}, u32[]{:S(2)}, u32[]{:S(2)}) async-start(bf16[32,320,144]{1,2,0:T(8,128)(2,1)} %stack.10), calls=%async_computation | async-start | bytes 7077888 | tf_op jit(solution)/shard_map/all_to_all | solution.py:41
  20.6 249.8 %reduce-scatter.4.cloned.1.call-start = ((), (), s32[]{:S(2)}) async-start(), calls=%async_computation.2 | async-start | bytes 3649536
  102.2 26.7 %copy-start.2 = (bf16[320,128]{1,0:T(8,128)(2,1)}, bf16[320,128]{1,0:T(8,128)(2,1)S(1)}, u32[]{:S(2)}) copy-start(bf16[320,128]{1,0:T(8,128)(2,1)S(1)} %fusion.10) | copy-start | bytes 245764
  102.2 14.8 %collective-permute-start = (bf16[320,128]{1,0:T(8,128)(2,1)S(1)}, bf16[320,128]{1,0:T(8,128)(2,1)S(1)}, u32[]{:S(2)}, u32[]{:S(2)}) collective-permute-start(bf16[320,128]{1,0:T(8,128)(2,1)S(1)} %fusion.10), channel_id=1, source_target_pairs={{0,128},{32,160},{64,192},{96,224},{128,256},{160,288},{192,320},{... | collective-permute-start | bytes 245768 | tf_op jit(solution)/shard_map/ppermute | solution.py:16
  117.1 11.9 %collective-permute-start.1 = (bf16[320,128]{1,0:T(8,128)(2,1)S(1)}, bf16[320,128]{1,0:T(8,128)(2,1)S(1)}, u32[]{:S(2)}, u32[]{:S(2)}) collective-permute-start(bf16[320,128]{1,0:T(8,128)(2,1)S(1)} %collective-permute-done), channel_id=1, source_target_pairs={{0,128},{32,160},{64,192},{96,224},{128,256},{160,288},{192,320},{... | collective-permute-start | bytes 245768 | tf_op jit(solution)/shard_map/ppermute | solution.py:16
  273.0 0.7 copy-start.1
  274.4 7.6 %collective-permute-start.2 = (bf16[160,144]{1,0:T(8,128)(2,1)}, bf16[160,144]{1,0:T(8,128)(2,1)}, u32[]{:S(2)}, u32[]{:S(2)}) collective-permute-start(bf16[160,144]{1,0:T(8,128)(2,1)} %select_convert_fusion), channel_id=1, source_target_pairs={{0,64},{32,96},{64,0},{96,32},{128,192},{160,224},{192,128},{224,1... | collective-permute-start | bytes 138248 | tf_op jit(solution)/shard_map/ppermute | solution.py:10
  283.0 5.9 %collective-permute-start.3 = (bf16[80,144]{1,0:T(8,128)(2,1)S(1)}, bf16[80,144]{1,0:T(8,128)(2,1)S(1)}, u32[]{:S(2)}, u32[]{:S(2)}) collective-permute-start(bf16[80,144]{1,0:T(8,128)(2,1)S(1)} %select_convert_fusion.1), channel_id=1, source_target_pairs={{0,32},{32,0},{64,96},{96,64},{128,160},{160,128},{192,224},{224,1... | collective-permute-start | bytes 69128 | tf_op jit(solution)/shard_map/ppermute | solution.py:10
Sparse Core Ops, SparseCore 0:
  137.9 132.4 reduce-scatter.3
